TPU v7x, 32 devices: a whole 2x2x4 slice. The times are simulated.
32 devices in a mesh: seq: 8 (over y, x, core), wsh: 4 (over z).
Axes of the slice: x: 2, y: 2, z: 4, core: 2. Of those that a mesh axis runs over, the one named last changes fastest.
Arguments:
- x_in: bfloat16 [4, 4096, 1024], P('wsh', 'seq'), may hold values from -6 to 6
- seg_ids: int32 [4, 4096], P('wsh', 'seq'), may hold values from 0 to 7, never falling along the last dimension, each value on 1 to 2048 neighbouring positions
- in_weight: bfloat16 [1024, 4384], P('wsh'), may hold values from -0.1875 to 0.1875
- out_weight: bfloat16 [2048, 1024], P('wsh'), may hold values from -0.125 to 0.125
- conv_weight: bfloat16 [4, 2304], P(None, 'wsh'), may hold values from -3 to 3
- conv_bias: bfloat16 [2304], P('wsh'), may hold values from -0.5 to 0.5
- dt_bias: bfloat16 [32], P('wsh'), may hold values from -6 to -3
- a_log: bfloat16 [32], P('wsh'), may hold values from -4 to 1.5
- skip_gain: bfloat16 [32], P('wsh'), may hold values from 0.5 to 1.5
- norm_gain: bfloat16 [1024], P('wsh'), may hold values from 0.5 to 1.5
- gate_gain: bfloat16 [2048], P('wsh'), may hold values from 0.5 to 1.5
- cotangent: bfloat16 [4, 4096, 1024], P('wsh', 'seq'), may hold values from -6 to 6
Outputs:
- output: bfloat16 [4, 4096, 1024], P('wsh', 'seq')
- grad_input: float32 [4, 4096, 1024], P('wsh', 'seq')
- grad_in_weight: float32 [1024, 4384], P('wsh')
- grad_out_weight: float32 [2048, 1024], P('wsh')
- grad_conv_weight: float32 [4, 2304], P(None, 'wsh')
- grad_conv_bias: float32 [2304], P('wsh')
- grad_dt_bias: float32 [32], P('wsh')
- grad_a_log: float32 [32], P('wsh')
- grad_skip: float32 [32], P('wsh')
- grad_norm_gain: float32 [1024], P('wsh')
- grad_gate_gain: float32 [2048], P('wsh')
Inputs may be any that keep to these rules, and one draw needn't show every extreme that they name: `seg_ids`: in each stream, document numbers never fall, each document has 1 to 2048 rows and one has exactly 2048.
All inputs are finite; a program needn't handle non-finite values.
Results may differ from a plain program's by a relative error of at most 0.012.
The roundings to bfloat16 on the way count: a program that leaves them out, or rounds other values in their place, can miss the bound.
Values may be sent and summed in bfloat16 or wider, within the bound.
No kernel may reach another device: no remote copies, remote signals or barrier semaphores. Data moves between devices by JAX's collectives and lax.ppermute only.
A program may use at most 192 MiB of HBM per device.

v0:
```python
import jax
import jax.numpy as jnp
from jax import lax
from jax.sharding import PartitionSpec as P

BLOCK = 512
epsilon = 1e-05
highest = lax.Precision.HIGHEST


def shifted(value, axis, steps):
    count = lax.axis_size(axis)
    first, last = (max(0, -steps), min(count, count - steps))
    return lax.ppermute(value, axis, [(source, source + steps) for source in range(first, last)])


def rms_scale(values, gain_vec):
    return (
        values * lax.rsqrt(jnp.mean(values * values, axis=-1, keepdims=True) + epsilon) * gain_vec
    )


def gated_norm(scanned, gate_part, gain_vec):
    return rms_scale(scanned * jax.nn.silu(gate_part), gain_vec)


def conv_silu(extended, ext_ids, conv_weight, conv_bias):
    tap_count = conv_weight.shape[0]
    rows_count = extended.shape[0] - tap_count + 1
    current = ext_ids[tap_count - 1 :]
    summed = jnp.zeros((rows_count, extended.shape[1]), jnp.float32) + conv_bias[None, :]
    for offset in range(tap_count):
        window = extended[offset : offset + rows_count]
        matching = (ext_ids[offset : offset + rows_count] == current).astype(jnp.float32)
        summed = summed + window * conv_weight[offset][None, :] * matching[:, None]
    return jax.nn.silu(summed)


def scan_heads(head_x, head_dt, b_rows, c_rows, segment_ids, dt_bias, a_log, skip_gain, block_rows):
    length = head_x.shape[0]
    head_count = head_dt.shape[1]
    head_dim = head_x.shape[1] // head_count
    state_dim = b_rows.shape[1]
    blocks = length // block_rows
    step_size = jax.nn.softplus(head_dt + dt_bias[None, :])
    log_decay = -jnp.exp(a_log)[None, :] * step_size
    x_heads = head_x.reshape(length, head_count, head_dim)
    scaled = x_heads * step_size[:, :, None]
    prev_ids = jnp.concatenate(
        [jnp.full((1,), -1, jnp.int32), segment_ids[block_rows - 1 :: block_rows][:-1]]
    )
    lower_mask = jnp.tril(jnp.ones((block_rows, block_rows), jnp.bool_))

    def one_block(carry_state, pieces):
        decay_part, scaled_part, b_part, c_part, id_part, prev_id = pieces
        cumulative = jnp.cumsum(decay_part, axis=0)
        linked = (id_part[:, None] == id_part[None, :]) & lower_mask
        differ = cumulative.T[:, :, None] - cumulative.T[:, None, :]
        kernel = jnp.where(linked[None], jnp.exp(jnp.where(linked[None], differ, 0.0)), 0.0)
        scores = jnp.dot(c_part, b_part.T, precision=highest)
        mixed_kernel = kernel * scores[None]
        intra_out = jnp.einsum("hts,shp->thp", mixed_kernel, scaled_part, precision=highest)
        carried = (id_part == prev_id).astype(jnp.float32)
        carry_in = jnp.exp(cumulative) * carried[:, None]
        inter_out = (
            jnp.einsum("tn,hpn->thp", c_part, carry_state, precision=highest) * carry_in[:, :, None]
        )
        end_link = (id_part == id_part[-1]).astype(jnp.float32)
        to_end = jnp.exp(cumulative[-1][None, :] - cumulative) * end_link[:, None]
        fresh = jnp.einsum(
            "shp,sn->hpn", to_end[:, :, None] * scaled_part, b_part, precision=highest
        )
        block_decay = jnp.exp(cumulative[-1]) * carried[-1]
        new_state = carry_state * block_decay[:, None, None] + fresh
        return (new_state, intra_out + inter_out)

    pieces = (
        log_decay.reshape(blocks, block_rows, head_count),
        scaled.reshape(blocks, block_rows, head_count, head_dim),
        b_rows.reshape(blocks, block_rows, state_dim),
        c_rows.reshape(blocks, block_rows, state_dim),
        segment_ids.reshape(blocks, block_rows),
        prev_ids,
    )
    initial = jnp.zeros((head_count, head_dim, state_dim), jnp.float32)
    ignored, outputs = lax.scan(jax.checkpoint(one_block), initial, pieces)
    result = outputs.reshape(length, head_count, head_dim) + skip_gain[None, :, None] * x_heads
    return result.reshape(length, head_count * head_dim)


def local(
    x_in,
    seg_ids,
    in_weight,
    out_weight,
    conv_weight,
    conv_bias,
    dt_bias,
    a_log,
    skip_gain,
    norm_gain,
    gate_gain,
    cotangent,
):
    w_in, w_out, conv_full, bias_full, dt_full, alog_full, skip_full, norm_full, gate_full = (
        lax.all_gather(in_weight, "wsh", axis=0, tiled=True),
        lax.all_gather(out_weight, "wsh", axis=0, tiled=True),
        lax.all_gather(conv_weight, "wsh", axis=1, tiled=True),
        lax.all_gather(conv_bias, "wsh", axis=0, tiled=True),
        lax.all_gather(dt_bias, "wsh", axis=0, tiled=True),
        lax.all_gather(a_log, "wsh", axis=0, tiled=True),
        lax.all_gather(skip_gain, "wsh", axis=0, tiled=True),
        lax.all_gather(norm_gain, "wsh", axis=0, tiled=True),
        lax.all_gather(gate_gain, "wsh", axis=0, tiled=True),
    )
    tok_rows = x_in.shape[1]
    seq_count = lax.axis_size("seq")
    seq_index = lax.axis_index("seq")
    row_start = seq_index * tok_rows
    inner_width = w_out.shape[0]
    head_count = dt_full.shape[0]
    state_dim = (w_in.shape[1] - 2 * inner_width - head_count) // 2
    channels = inner_width + 2 * state_dim
    tap_count = conv_full.shape[0]
    residual_in = x_in[0].astype(jnp.float32)
    ids_full = lax.all_gather(seg_ids, "seq", axis=1, tiled=True)[0]
    normed_f, norm_pull = jax.vjp(rms_scale, residual_in, norm_full.astype(jnp.float32))
    normed = normed_f.astype(jnp.bfloat16)
    projected = jnp.dot(normed, w_in, preferred_element_type=jnp.float32).astype(jnp.bfloat16)
    gate_part = projected[:, :inner_width]
    conv_in = projected[:, inner_width : inner_width + channels]
    dt_part = projected[:, inner_width + channels :]
    halo_rows = shifted(conv_in[tok_rows - (tap_count - 1) :], "seq", 1)
    extended = jnp.concatenate([halo_rows, conv_in]).astype(jnp.float32)
    padded_ids = jnp.concatenate([jnp.full((tap_count - 1,), -1, jnp.int32), ids_full])
    ext_ids = lax.dynamic_slice_in_dim(padded_ids, row_start, tok_rows + tap_count - 1)

    def conv_local(ext_rows, weights, biases):
        return conv_silu(ext_rows, ext_ids, weights, biases)

    activated, conv_pull = jax.vjp(
        conv_local, extended, conv_full.astype(jnp.float32), bias_full.astype(jnp.float32)
    )
    x_part = activated[:, :inner_width].astype(jnp.bfloat16)
    bc_part = activated[:, inner_width:].astype(jnp.bfloat16)
    head_x, head_dt = (
        lax.all_to_all(x_part, "seq", split_axis=1, concat_axis=0, tiled=True),
        lax.all_to_all(dt_part, "seq", split_axis=1, concat_axis=0, tiled=True),
    )
    bc_full = lax.all_gather(bc_part, "seq", axis=0, tiled=True)
    local_heads = head_count // seq_count
    head_start = seq_index * local_heads
    dt_local = lax.dynamic_slice_in_dim(dt_full, head_start, local_heads).astype(jnp.float32)
    alog_local = lax.dynamic_slice_in_dim(alog_full, head_start, local_heads).astype(jnp.float32)
    skip_local = lax.dynamic_slice_in_dim(skip_full, head_start, local_heads).astype(jnp.float32)

    def scan_local(x_vals, dt_vals, b_vals, c_vals, bias_vals, decay_vals, skip_vals):
        return scan_heads(
            x_vals, dt_vals, b_vals, c_vals, ids_full, bias_vals, decay_vals, skip_vals, BLOCK
        )

    scanned, scan_pull = jax.vjp(
        scan_local,
        head_x.astype(jnp.float32),
        head_dt.astype(jnp.float32),
        bc_full[:, :state_dim].astype(jnp.float32),
        bc_full[:, state_dim:].astype(jnp.float32),
        dt_local,
        alog_local,
        skip_local,
    )
    y_rows = lax.all_to_all(
        scanned.astype(jnp.bfloat16), "seq", split_axis=0, concat_axis=1, tiled=True
    )
    gated_f, gated_pull = jax.vjp(
        gated_norm,
        y_rows.astype(jnp.float32),
        gate_part.astype(jnp.float32),
        gate_full.astype(jnp.float32),
    )
    gated = gated_f.astype(jnp.bfloat16)
    output = (residual_in + jnp.dot(gated, w_out, preferred_element_type=jnp.float32)).astype(
        jnp.bfloat16
    )
    grad_out = cotangent[0]
    grad_wout = lax.dot_general(
        gated, grad_out, (((0,), (0,)), ((), ())), preferred_element_type=jnp.float32
    )
    grad_gated = lax.dot_general(
        grad_out, w_out, (((1,), (1,)), ((), ())), preferred_element_type=jnp.float32
    )
    grad_y, grad_gate_part, grad_gate_gain = gated_pull(grad_gated)
    head_grad = lax.all_to_all(
        grad_y.astype(jnp.bfloat16), "seq", split_axis=1, concat_axis=0, tiled=True
    )
    grad_hx, grad_hdt, grad_b, grad_c, grad_bias, grad_decay, grad_skipped = scan_pull(
        head_grad.astype(jnp.float32)
    )
    back_x, back_dt = (
        lax.all_to_all(
            grad_hx.astype(jnp.bfloat16), "seq", split_axis=0, concat_axis=1, tiled=True
        ),
        lax.all_to_all(
            grad_hdt.astype(jnp.bfloat16), "seq", split_axis=0, concat_axis=1, tiled=True
        ),
    )
    grad_bc = lax.psum_scatter(
        jnp.concatenate([grad_b, grad_c], axis=1).astype(jnp.bfloat16),
        "seq",
        scatter_dimension=0,
        tiled=True,
    ).astype(jnp.float32)
    grad_act = jnp.concatenate([back_x.astype(jnp.float32), grad_bc], axis=1)
    grad_ext, grad_convw, grad_convb = conv_pull(grad_act)
    rim_back = shifted(grad_ext[: tap_count - 1], "seq", -1)
    grad_conv_in = jnp.concatenate(
        [grad_ext[tap_count - 1 : tok_rows], grad_ext[tok_rows:] + rim_back]
    )
    grad_proj = jnp.concatenate(
        [grad_gate_part, grad_conv_in, back_dt.astype(jnp.float32)], axis=1
    ).astype(jnp.bfloat16)
    grad_win = lax.dot_general(
        normed, grad_proj, (((0,), (0,)), ((), ())), preferred_element_type=jnp.float32
    )
    grad_normed = lax.dot_general(
        grad_proj, w_in, (((1,), (1,)), ((), ())), preferred_element_type=jnp.float32
    )
    grad_resid, grad_norm = norm_pull(grad_normed)
    grad_input = grad_resid + grad_out.astype(jnp.float32)

    def place_heads(values):
        return lax.dynamic_update_slice_in_dim(
            jnp.zeros((head_count,), jnp.float32), values, head_start, 0
        )

    grad_dtb = place_heads(grad_bias)
    grad_alog = place_heads(grad_decay)
    grad_skip = place_heads(grad_skipped)
    summed = lax.psum(
        (
            grad_win,
            grad_wout,
            grad_convw,
            grad_convb,
            grad_dtb,
            grad_alog,
            grad_skip,
            grad_norm,
            grad_gate_gain,
        ),
        "seq",
    )
    shards = (
        lax.psum_scatter(summed[0], "wsh", scatter_dimension=0, tiled=True),
        lax.psum_scatter(summed[1], "wsh", scatter_dimension=0, tiled=True),
        lax.psum_scatter(summed[2], "wsh", scatter_dimension=1, tiled=True),
        lax.psum_scatter(summed[3], "wsh", scatter_dimension=0, tiled=True),
        lax.psum_scatter(summed[4], "wsh", scatter_dimension=0, tiled=True),
        lax.psum_scatter(summed[5], "wsh", scatter_dimension=0, tiled=True),
        lax.psum_scatter(summed[6], "wsh", scatter_dimension=0, tiled=True),
        lax.psum_scatter(summed[7], "wsh", scatter_dimension=0, tiled=True),
        lax.psum_scatter(summed[8], "wsh", scatter_dimension=0, tiled=True),
    )
    return (
        output[None],
        grad_input[None],
        shards[0],
        shards[1],
        shards[2],
        shards[3],
        shards[4],
        shards[5],
        shards[6],
        shards[7],
        shards[8],
    )


def solution(mesh):
    in_specs = (
        P("wsh", "seq", None),
        P("wsh", "seq"),
        P("wsh", None),
        P("wsh", None),
        P(None, "wsh"),
        P("wsh"),
        P("wsh"),
        P("wsh"),
        P("wsh"),
        P("wsh"),
        P("wsh"),
        P("wsh", "seq", None),
    )
    out_specs = (
        P("wsh", "seq", None),
        P("wsh", "seq", None),
        P("wsh", None),
        P("wsh", None),
        P(None, "wsh"),
        P("wsh"),
        P("wsh"),
        P("wsh"),
        P("wsh"),
        P("wsh"),
        P("wsh"),
    )
    return jax.shard_map(local, mesh=mesh, in_specs=in_specs, out_specs=out_specs, check_vma=False)
```

profile of v0, /device:TPU:0, one launch (start us, length us, event | category | flops | bytes accessed | tf_op | source)
XLA Modules:
  0.0 1654.8 jit_solution(10845675449132418567)
XLA Ops:
  8.6 12.6 all-gather
  21.3 31.8 %all-gather.1 = bf16[4,576,4]{1,2,0:T(4,128)(2,1)S(1)} all-gather(bf16[1,576,4]{1,2,0:T(4,128)(2,1)} %bitcast.442), channel_id=1, replica_groups=mesh['seq'=8,'wsh'=4] {'wsh'}, dimensions={0}, use_global_device_ids=true | all-gather | bytes 23040 | tf_op jit(solution)/shard_map/all_gather | solution.py:108
  53.2 9.0 all_gather.37
  63.9 107.3 %all-gather.7.cloned.1.call-done = bf16[1024,4384]{0,1:T(8,128)(2,1)} async-done(((bf16[256,4384]{0,1:T(8,128)(2,1)}), bf16[1024,4384]{0,1:T(8,128)(2,1)}) %all-gather.7.cloned.1.call-update) | async-done | bytes 8978448 | tf_op jit(solution)/shard_map/all_gather | solution.py:106
  171.3 9.2 convolution_convert_fusion
  187.3 9.5 all-reduce.24
  222.2 27.8 %all-to-all-done.1 = bf16[512,8,256]{0,2,1:T(8,128)(2,1)S(1)} async-done(((bf16[512,8,256]{0,2,1:T(8,128)(2,1)}), bf16[512,8,256]{0,2,1:T(8,128)(2,1)S(1)}, u32[]{:S(2)}, u32[]{:S(2)}) %all-to-all-start.1) | async-done | bytes 2097184 | tf_op jit(solution)/shard_map/all_to_all | solution.py:147
  262.3 271.7 %while.40 = (s32[]{:T(128)}, f32[4,64,128]{2,1,0:T(8,128)S(1)}, f32[8,512,4,64]{1,0,3,2:T(8,128)}, f32[8,4,64,128]{3,2,1,0:T(8,128)}, f32[8,512,4]{1,2,0:T(4,128...) while((s32[]{:T(128)}, f32[4,64,128]{2,1,0:T(8,128)S(1)}, ...), condition=%wide.region_4.5_spmd.clone, body=%wide.region_1.4_spmd.clone.sunk | while | flops 1616420864 | bytes 9202848 | solution.py:86
  284.8 11.5 dynamic_update_slice.83
  318.8 11.5 dynamic_update_slice.83
  352.7 11.5 dynamic_update_slice.83
  386.7 11.5 dynamic_update_slice.83
  420.6 11.5 dynamic_update_slice.83
  454.6 11.5 dynamic_update_slice.83
  488.5 11.5 dynamic_update_slice.83
  522.5 11.5 dynamic_update_slice.83
  543.2 11.9 all-gather.2
  555.1 14.6 all-to-all-done.2
  584.4 7.0 multiply_reduce_fusion.7
  603.2 26.5 %all-to-all-done.3 = bf16[512,8,256]{0,2,1:T(8,128)(2,1)S(1)} async-done(((bf16[512,8,256]{0,2,1:T(8,128)(2,1)}), bf16[512,8,256]{0,2,1:T(8,128)(2,1)S(1)}, u32[]{:S(2)}, u32[]{:S(2)}) %all-to-all-start.3) | async-done | bytes 2097184 | tf_op jit(solution)/shard_map/all_to_all | solution.py:193
  638.3 369.4 %while.41 = (s32[]{:T(128)}, f32[4,64,128]{2,1,0:T(8,128)S(1)}, f32[8,512,4]{1,2,0:T(4,128)}, f32[8,512,4,64]{1,3,2,0:T(8,128)}, bf16[8,512,128]{2,1,0:T(8,128)(...) while((s32[]{:T(128)}, f32[4,64,128]{2,1,0:T(8,128)S(1)}, ...), condition=%wide.region_19.20_spmd.clone, body=%wide.region_7.19_spmd.clone.sunk | while | flops 3843487744 | bytes 28192232 | solution.py:86
  1011.0 7.9 fusion.115
  1050.1 26.4 %all-to-all-done.4 = bf16[8,512,256]{1,2,0:T(8,128)(2,1)} async-done(((bf16[8,512,256]{1,2,0:T(8,128)(2,1)}), bf16[8,512,256]{1,2,0:T(8,128)(2,1)}, u32[]{:S(2)}, u32[]{:S(2)}) %all-to-all-start.4) | async-done | bytes 2097184 | tf_op jit(solution)/shard_map/all_to_all | solution.py:200
  1080.5 12.2 multiply_reduce_fusion.6
  1101.4 10.3 fusion.119
  1115.9 80.4 %reduce-scatter.11.cloned.1.call-done = f32[512,1024]{1,0:T(8,128)} async-done(((f32[2048,1024]{1,0:T(8,128)}), f32[512,1024]{1,0:T(8,128)}) %reduce-scatter.11.cloned.1.call-update) | async-done | bytes 2097168 | tf_op jit(solution)/shard_map/reduce_scatter | solution.py:255
  1196.3 302.1 %reduce-scatter.9.cloned.1.call-done = f32[256,4384]{0,1:T(8,128)} async-done(((f32[1024,4384]{0,1:T(8,128)}), f32[256,4384]{0,1:T(8,128)}) %reduce-scatter.9.cloned.1.call-update) | async-done | bytes 4489232 | tf_op jit(solution)/shard_map/reduce_scatter | solution.py:254
  1498.4 7.2 fusion.114
  1510.0 11.8 fusion.107
  1521.8 18.7 %all-reduce.23 = (f32[2304]{0:T(1024)S(1)}, f32[32]{0:T(128)S(1)}, f32[32]{0:T(128)S(1)}, f32[32]{0:T(128)S(1)}, f32[1024]{0:T(1024)S(1)}, /*index=5*/f32[2048]{0:T(1024)S(1)}) all-reduce(f32[2304]{0:T(1024)S(1)} %get-tuple-element.698, f32[32]{0:T(128)S(1)} %dynamic_update_slice.61, ...), channel_id=6, replica_groups=mesh['seq'=8,'wsh'=4] {'wsh'}, use_global_device_ids=true, to_apply=%region_35.36.clone | all-reduce | flops 5472 | bytes 43776
  1545.6 24.4 %all-reduce.21 = (f32[4,576]{1,0:T(4,128)}, f32[576]{0:T(1024)}, f32[8]{0:T(128)}, f32[8]{0:T(128)}, f32[8]{0:T(128)}, /*index=5*/f32[256]{0:T(256)}, f32[512]{0:T(512)}) all-reduce(f32[4,576]{1,0:T(4,128)S(1)} %copy.188, f32[576]{0:T(1024)S(1)} %dynamic-slice.5, f32[8]{0:T(128)S(1)} %dynamic-slice.7, ...), channel_id=1, replica_groups=mesh['seq'=8,'wsh'=4] {'seq'}, use_global_device_ids=true, to_apply=%region_31.32 | all-reduce | flops 3672 | bytes 29376 | tf_op jit(solution)/shard_map/psum | solution.py:239
  1570.0 71.6 %all-reduce.27.cloned.1.call-done = (f32[256,4384]{0,1:T(8,128)}, f32[512,1024]{1,0:T(8,128)}) async-done(((f32[256,4384]{0,1:T(8,128)}, f32[512,1024]{1,0:T(8,128)}), (f32[256,4384]{0,1:T(8,128)}, f32[512,1024]{1,0:T(8,128)})) %all-reduce.27.cloned.1.call-update) | async-done | bytes 6586384 | tf_op jit(solution)/shard_map/psum | solution.py:239
  (859 shorter events, 701.1 us)
Async XLA Ops:
  7.2 164.1 %all-gather.7.cloned.1.call-start = ((), (), s32[]{:S(2)}) async-start(), calls=%async_computation.10 | async-start | bytes 11223040 | tf_op jit(solution)/shard_map/all_gather | solution.py:106
  7.9 249.8 %all-gather.9.cloned.1.call-start = ((), (), s32[]{:S(2)}) async-start(), calls=%async_computation.11 | async-start | bytes 2359296 | tf_op jit(solution)/shard_map/all_gather | solution.py:150
  21.3 159.2 %copy-start.47 = (f32[4,1,256]{2,1,0:T(1,128)}, f32[4,1,256]{2,1,0:T(1,128)S(1)}, u32[]{:S(2)}) copy-start(f32[4,1,256]{2,1,0:T(1,128)S(1)} %convert_element_type.252) | copy-start | bytes 12292
  63.8 116.7 %copy-start.45 = (f32[512]{0:T(512)}, f32[512]{0:T(512)S(1)}, u32[]{:S(2)}) copy-start(f32[512]{0:T(512)S(1)} %fusion.110) | copy-start | bytes 6148
  63.8 116.7 %copy-start.51 = (f32[512]{0:T(512)}, f32[512]{0:T(512)S(1)}, u32[]{:S(2)}) copy-start(f32[512]{0:T(512)S(1)} %fusion.134) | copy-start | bytes 6148
  63.9 133.4 %copy-start.37 = (f32[512]{0:T(512)}, f32[512]{0:T(512)S(1)}, u32[]{:S(2)}) copy-start(f32[512]{0:T(512)S(1)} %get-tuple-element.812) | copy-start | bytes 6148
  63.9 133.5 %copy-start.39 = (f32[512]{0:T(512)}, f32[512]{0:T(512)S(1)}, u32[]{:S(2)}) copy-start(f32[512]{0:T(512)S(1)} %get-tuple-element.813) | copy-start | bytes 6148
  63.9 133.5 %copy-start.41 = (f32[512]{0:T(512)}, f32[512]{0:T(512)S(1)}, u32[]{:S(2)}) copy-start(f32[512]{0:T(512)S(1)} %get-tuple-element.814) | copy-start | bytes 6148
  182.8 14.0 collective-permute-start
  204.3 9.4 all-to-all-start
  213.6 37.6 %copy-start.23 = (bf16[512,8,4]{0,2,1:T(4,128)(2,1)}, bf16[512,8,4]{0,2,1:T(4,128)(2,1)S(1)}, u32[]{:S(2)}) copy-start(bf16[512,8,4]{0,2,1:T(4,128)(2,1)S(1)} %all-to-all-done) | copy-start | bytes 98308
  213.6 36.4 %all-to-all-start.1 = ((bf16[512,8,256]{0,2,1:T(8,128)(2,1)}), bf16[512,8,256]{0,2,1:T(8,128)(2,1)S(1)}, u32[]{:S(2)}, u32[]{:S(2)}) async-start(bf16[512,8,256]{0,2,1:T(8,128)(2,1)} %bitcast.407), calls=%async_computation.1 | async-start | bytes 4194304 | tf_op jit(solution)/shard_map/all_to_all | solution.py:147
  217.8 366.5 %all-gather.11.cloned.1.call-start = ((), (), s32[]{:S(2)}) async-start(), calls=%async_computation.12 | async-start | bytes 5242880 | tf_op jit(solution)/shard_map/all_gather | solution.py:107
  220.7 313.3 %copy-start.49 = (f32[256]{0:T(256)}, f32[256]{0:T(256)S(1)}, u32[]{:S(2)}) copy-start(f32[256]{0:T(256)S(1)} %mul.804) | copy-start | bytes 3076
  220.8 36.9 %copy-start.56 = (f32[4]{0:T(128)}, f32[4]{0:T(128)S(1)}, u32[]{:S(2)}) copy-start(f32[4]{0:T(128)S(1)} %fusion.136) | copy-start | bytes 52
  220.9 36.8 %copy-start.54 = (f32[4]{0:T(128)}, f32[4]{0:T(128)S(1)}, u32[]{:S(2)}) copy-start(f32[4]{0:T(128)S(1)} %dynamic-slice_convert_fusion.1) | copy-start | bytes 52
  222.2 35.4 %copy-start.21 = (f32[8,512,4]{1,2,0:T(4,128)}, f32[8,512,4]{1,2,0:T(4,128)S(1)}, u32[]{:S(2)}) copy-start(f32[8,512,4]{1,2,0:T(4,128)S(1)} %get-tuple-element.780) | copy-start | bytes 196612
  250.0 284.0 %copy-start.6 = (bf16[512,8,256]{0,2,1:T(8,128)(2,1)}, bf16[512,8,256]{0,2,1:T(8,128)(2,1)S(1)}, u32[]{:S(2)}) copy-start(bf16[512,8,256]{0,2,1:T(8,128)(2,1)S(1)} %all-to-all-done.1) | copy-start | bytes 6291460
  539.5 30.2 %all-to-all-start.2 = ((bf16[8,512,256]{1,2,0:T(8,128)(2,1)}), bf16[8,512,256]{1,2,0:T(8,128)(2,1)S(1)}, u32[]{:S(2)}, u32[]{:S(2)}) async-start(bf16[8,512,256]{1,2,0:T(8,128)(2,1)} %copy.172), calls=%async_computation.2 | async-start | bytes 4194304 | tf_op jit(solution)/shard_map/all_to_all | solution.py:172
  555.1 36.3 %copy-start.27 = (f32[4,1,512]{2,1,0:T(1,128)}, f32[4,1,512]{2,1,0:T(1,128)S(1)}, u32[]{:S(2)}) copy-start(f32[4,1,512]{2,1,0:T(1,128)S(1)} %convert_element_type.254) | copy-start | bytes 24580
  599.5 30.2 %all-to-all-start.3 = ((bf16[512,8,256]{0,2,1:T(8,128)(2,1)}), bf16[512,8,256]{0,2,1:T(8,128)(2,1)S(1)}, u32[]{:S(2)}, u32[]{:S(2)}) async-start(bf16[512,8,256]{0,2,1:T(8,128)(2,1)} %bitcast.408), calls=%async_computation.3 | async-start | bytes 4194304 | tf_op jit(solution)/shard_map/all_to_all | solution.py:193
  603.1 477.3 %reduce-scatter.7.cloned.1.call-start = ((), (), s32[]{:S(2)}) async-start(), calls=%async_computation.13 | async-start | bytes 2359296 | tf_op jit(solution)/shard_map/reduce_scatter | solution.py:207
  1011.0 185.3 %reduce-scatter.11.cloned.1.call-start = ((), (), s32[]{:S(2)}) async-start(), calls=%async_computation.15 | async-start | bytes 10485760 | tf_op jit(solution)/shard_map/reduce_scatter | solution.py:255
  1034.6 10.9 all-to-all-start.5
  1045.5 34.9 %copy-start.38 = (f32[512]{0:T(512)S(1)}, f32[512]{0:T(512)}, u32[]{:S(2)}) copy-start(f32[512]{0:T(512)} %copy-done.37) | copy-start | bytes 6148
  1045.5 34.9 %copy-start.40 = (f32[512]{0:T(512)S(1)}, f32[512]{0:T(512)}, u32[]{:S(2)}) copy-start(f32[512]{0:T(512)} %copy-done.39) | copy-start | bytes 6148
  1045.5 34.9 %copy-start.42 = (f32[512]{0:T(512)S(1)}, f32[512]{0:T(512)}, u32[]{:S(2)}) copy-start(f32[512]{0:T(512)} %copy-done.41) | copy-start | bytes 6148
  1045.5 31.0 %all-to-all-start.4 = ((bf16[8,512,256]{1,2,0:T(8,128)(2,1)}), bf16[8,512,256]{1,2,0:T(8,128)(2,1)}, u32[]{:S(2)}, u32[]{:S(2)}) async-start(bf16[8,512,256]{1,2,0:T(8,128)(2,1)} %copy.178), calls=%async_computation.4 | async-start | bytes 4194304 | tf_op jit(solution)/shard_map/all_to_all | solution.py:200
  1049.9 448.5 %reduce-scatter.9.cloned.1.call-start = ((), (), s32[]{:S(2)}) async-start(), calls=%async_computation.14 | async-start | bytes 22446080 | tf_op jit(solution)/shard_map/reduce_scatter | solution.py:254
  1094.6 4.0 collective-permute-start.1
  1111.7 432.8 %reduce-scatter.13.cloned.1.call-start = ((), (), s32[]{:S(2)}) async-start(), calls=%async_computation.16 | async-start | bytes 1474560
  1113.3 528.3 %all-reduce.27.cloned.1.call-start = ((), (), s32[]{:S(2)}) async-start(), calls=%async_computation.17 | async-start | bytes 13172736 | tf_op jit(solution)/shard_map/psum | solution.py:239
  (80 other events, 653.8 us)
Sparse Core Ops, SparseCore 0:
  9.5 161.6 all-gather.6
  203.7 38.2 all-gather.8
  243.6 79.8 all-gather.10
  1011.1 38.2 reduce-scatter.6
  1051.6 144.6 reduce-scatter.10
  1198.5 299.8 reduce-scatter.8
  1500.7 30.4 reduce-scatter.12
  1534.7 106.8 all-reduce.26
where the time goes:
time: 1670 us; the launch traced here: 1650 us
  waiting for transfers between devices  658 us (39%)
  matrix products  320 us (19%)
  local copies, waits for them, and re-layouts  300 us (18%)
  other arithmetic  211 us (13%)
  blocking collectives  118 us (7%)
  starting transfers between devices  26.4 us (2%)
  between operations  19.3 us (1%)
    reduce_scatter x1, waiting for transfers between devices, local(): lax.psum_scatter(summed[0], 'wsh', scatter_dimension=0, tiled=True)  302 us
    dot_general x24, matrix products, one_block(): jnp.einsum('hts,shp->thp', mixed_kernel, scaled_part, precision=highest)  145 us
    all_gather x1, waiting for transfers between devices, local(): lax.all_gather(in_weight, 'wsh', axis=0, tiled=True)  107 us
    dynamic_update_slice x24, local copies, waits for them, and re-layouts, scan_heads(): ignored, outputs = lax.scan(jax.checkpoint(one_block), initial, pieces)  101 us
    another operation x60, other arithmetic  90.8 us
    reduce_scatter x1, waiting for transfers between devices, local(): lax.psum_scatter(summed[1], 'wsh', scatter_dimension=0, tiled=True)  80.4 us
    psum x1, waiting for transfers between devices, local(): lax.psum((grad_win, grad_wout, grad_convw, grad_convb, grad_dtb, grad_alo...  71.6 us
    dot_general x32, matrix products, one_block(): scores = jnp.dot(c_part, b_part.T, precision=highest)  64.9 us
  transfers between devices with their start and end apart: 16, of which 8 were waited for; matrix products, arithmetic and copies ran while one was open for 25% of the time, Pallas kernels for 0%

commit v1 on v0

--- a/solution.py
+++ b/solution.py
@@ -6,6 +6,12 @@
 BLOCK = 512
 epsilon = 1e-05
 highest = lax.Precision.HIGHEST
+
+
+def exchange_blocks(shard, name, split, join):
+    pieces = jnp.split(shard, lax.axis_size(name), axis=split)
+    received = lax.all_to_all(jnp.stack(pieces), name, 0, 0)
+    return jnp.concatenate(received, axis=join)
 
 
 def shifted(value, axis, steps):
@@ -144,7 +150,7 @@
     x_part = activated[:, :inner_width].astype(jnp.bfloat16)
     bc_part = activated[:, inner_width:].astype(jnp.bfloat16)
     head_x, head_dt = (
-        lax.all_to_all(x_part, "seq", split_axis=1, concat_axis=0, tiled=True),
+        exchange_blocks(x_part, "seq", 1, 0),
         lax.all_to_all(dt_part, "seq", split_axis=1, concat_axis=0, tiled=True),
     )
     bc_full = lax.all_gather(bc_part, "seq", axis=0, tiled=True)

time: 1670 us -> 1520 us (0.910)
  local copies, waits for them, and re-layouts: 300 us -> 158 us
    dynamic_update_slice x24 -> x8, local copies, waits for them, and re-layouts: 101 us -> 4.8 us  [scan_heads(): ignored, outputs = lax.scan(jax.checkpoint(one_block), initial, pieces)]
    dynamic_slice x40 -> x32, local copies, waits for them, and re-layouts: 52.8 us -> 9.72 us  [scan_heads(): ignored, outputs = lax.scan(jax.checkpoint(one_block), initial, pieces)]
    another operation x60 -> x59, other arithmetic: 90.8 us -> 91.4 us
  transfers between devices with their start and end apart: 16 -> 16, of which waited for: 8 -> 8; matrix products, arithmetic and copies ran while one was open for 25% -> 19% of each run, Pallas kernels for 0% -> 0%
where the time goes in v1:
time: 1520 us; the launch traced here: 1510 us
  waiting for transfers between devices  658 us (43%)
  matrix products  324 us (21%)
  other arithmetic  206 us (14%)
  local copies, waits for them, and re-layouts  158 us (10%)
  blocking collectives  119 us (8%)
  starting transfers between devices  26.4 us (2%)
  between operations  19.2 us (1%)
    reduce_scatter x1, waiting for transfers between devices, local(): lax.psum_scatter(summed[0], 'wsh', scatter_dimension=0, tiled=True)  302 us
    dot_general x24, matrix products, one_block(): jnp.einsum('hts,shp->thp', mixed_kernel, scaled_part, precision=highest)  149 us
    all_gather x1, waiting for transfers between devices, local(): lax.all_gather(in_weight, 'wsh', axis=0, tiled=True)  107 us
    another operation x59, other arithmetic  91.4 us
    reduce_scatter x1, waiting for transfers between devices, local(): lax.psum_scatter(summed[1], 'wsh', scatter_dimension=0, tiled=True)  78.7 us
    psum x1, waiting for transfers between devices, local(): lax.psum((grad_win, grad_wout, grad_convw, grad_convb, grad_dtb, grad_alo...  72.2 us
    dot_general x32, matrix products, one_block(): scores = jnp.dot(c_part, b_part.T, precision=highest)  56.9 us
    dot_general x32, matrix products, one_block(): jnp.einsum('tn,hpn->thp', c_part, carry_state, precision=highest)  37.7 us
  transfers between devices with their start and end apart: 16, of which 8 were waited for; matrix products, arithmetic and copies ran while one was open for 19% of the time, Pallas kernels for 0%

profile of v1, /device:TPU:0, one launch (start us, length us, event | category | flops | bytes accessed | tf_op | source)
XLA Modules:
  0.0 1512.7 jit_solution(9965487144411868096)
XLA Ops:
  8.6 12.6 all-gather
  21.3 31.8 %all-gather.1 = bf16[4,576,4]{1,2,0:T(4,128)(2,1)S(1)} all-gather(bf16[1,576,4]{1,2,0:T(4,128)(2,1)} %bitcast.476), channel_id=1, replica_groups=mesh['seq'=8,'wsh'=4] {'wsh'}, dimensions={0}, use_global_device_ids=true | all-gather | bytes 23040 | tf_op jit(solution)/shard_map/all_gather | solution.py:114
  53.2 9.0 all_gather.37
  64.5 106.8 %all-gather.7.cloned.1.call-done = bf16[1024,4384]{0,1:T(8,128)(2,1)} async-done(((bf16[256,4384]{0,1:T(8,128)(2,1)}), bf16[1024,4384]{0,1:T(8,128)(2,1)}) %all-gather.7.cloned.1.call-update) | async-done | bytes 8978448 | tf_op jit(solution)/shard_map/all_gather | solution.py:112
  171.3 9.3 convolution_convert_fusion
  187.3 9.5 all-reduce.24
  220.8 29.5 %all-to-all-done.1 = bf16[8,512,256]{2,1,0:T(8,128)(2,1)S(1)} async-done(((bf16[8,512,256]{2,1,0:T(8,128)(2,1)}), bf16[8,512,256]{2,1,0:T(8,128)(2,1)S(1)}, u32[]{:S(2)}, u32[]{:S(2)}) %all-to-all-start.1) | async-done | bytes 2097184 | tf_op jit(solution)/shard_map/all_to_all | solution.py:13
  265.6 157.4 %while.40 = (s32[]{:T(128)}, f32[4,64,128]{2,1,0:T(8,128)S(1)}, f32[8,512,4,64]{1,3,2,0:T(8,128)}, f32[8,4,64,128]{3,2,1,0:T(8,128)}, f32[8,512,4]{1,2,0:T(4,128...) while((s32[]{:T(128)}, f32[4,64,128]{2,1,0:T(8,128)S(1)}, ...), condition=%wide.region_4.5_spmd.clone, body=%wide.region_1.4_spmd.clone.sunk | while | flops 1616420864 | bytes 7107223 | solution.py:92
  270.2 6.8 fusion.216
  289.9 6.8 fusion.216
  309.6 6.8 fusion.216
  329.3 6.8 fusion.216
  348.9 6.8 fusion.216
  368.6 6.8 fusion.216
  388.3 6.8 fusion.216
  408.0 6.8 fusion.216
  436.2 12.1 all-gather.2
  448.4 14.4 all-to-all-done.2
  469.6 7.0 multiply_reduce_fusion.7
  487.4 26.5 %all-to-all-done.3 = bf16[512,8,256]{2,0,1:T(8,128)(2,1)S(1)} async-done(((bf16[512,8,256]{2,0,1:T(8,128)(2,1)}), bf16[512,8,256]{2,0,1:T(8,128)(2,1)S(1)}, u32[]{:S(2)}, u32[]{:S(2)}) %all-to-all-start.3) | async-done | bytes 2097184 | tf_op jit(solution)/shard_map/all_to_all | solution.py:199
  527.3 338.0 %while.41 = (s32[]{:T(128)}, f32[4,64,128]{2,1,0:T(8,128)S(1)}, f32[8,512,4]{1,2,0:T(4,128)}, f32[8,512,4,64]{1,3,2,0:T(8,128)}, bf16[8,512,128]{2,1,0:T(8,128)(...) while((s32[]{:T(128)}, f32[4,64,128]{2,1,0:T(8,128)S(1)}, ...), condition=%wide.region_19.20_spmd.clone, body=%wide.region_7.19_spmd.clone.sunk | while | flops 3843487744 | bytes 27799436 | solution.py:92
  868.6 7.9 fusion.113
  914.8 26.4 %all-to-all-done.4 = bf16[8,512,256]{2,1,0:T(8,128)(2,1)S(1)} async-done(((bf16[8,512,256]{2,1,0:T(8,128)(2,1)}), bf16[8,512,256]{2,1,0:T(8,128)(2,1)S(1)}, u32[]{:S(2)}, u32[]{:S(2)}) %all-to-all-start.4) | async-done | bytes 2097184 | tf_op jit(solution)/shard_map/all_to_all | solution.py:206
  942.9 12.1 multiply_reduce_fusion.6
  963.5 10.2 fusion.117
  975.5 78.7 %reduce-scatter.11.cloned.1.call-done = f32[512,1024]{1,0:T(8,128)} async-done(((f32[2048,1024]{1,0:T(8,128)}), f32[512,1024]{1,0:T(8,128)}) %reduce-scatter.11.cloned.1.call-update) | async-done | bytes 2097168 | tf_op jit(solution)/shard_map/reduce_scatter | solution.py:261
  1054.2 302.1 %reduce-scatter.9.cloned.1.call-done = f32[256,4384]{0,1:T(8,128)} async-done(((f32[1024,4384]{0,1:T(8,128)}), f32[256,4384]{0,1:T(8,128)}) %reduce-scatter.9.cloned.1.call-update) | async-done | bytes 4489232 | tf_op jit(solution)/shard_map/reduce_scatter | solution.py:260
  1358.9 6.8 fusion.112
  1366.6 11.8 fusion.105
  1378.3 19.2 %all-reduce.23 = (f32[2304]{0:T(1024)S(1)}, f32[32]{0:T(128)S(1)}, f32[32]{0:T(128)S(1)}, f32[32]{0:T(128)S(1)}, f32[1024]{0:T(1024)S(1)}, /*index=5*/f32[2048]{0:T(1024)S(1)}) all-reduce(f32[2304]{0:T(1024)S(1)} %get-tuple-element.684, f32[32]{0:T(128)S(1)} %dynamic_update_slice.61, ...), channel_id=6, replica_groups=mesh['seq'=8,'wsh'=4] {'wsh'}, use_global_device_ids=true, to_apply=%region_35.36.clone | all-reduce | flops 5472 | bytes 43776
  1402.6 24.6 %all-reduce.21 = (f32[4,576]{1,0:T(4,128)}, f32[576]{0:T(1024)}, f32[8]{0:T(128)}, f32[8]{0:T(128)}, f32[8]{0:T(128)}, /*index=5*/f32[256]{0:T(256)}, f32[512]{0:T(512)}) all-reduce(f32[4,576]{1,0:T(4,128)S(1)} %copy.143, f32[576]{0:T(1024)S(1)} %dynamic-slice.5, f32[8]{0:T(128)S(1)} %dynamic-slice.7, ...), channel_id=1, replica_groups=mesh['seq'=8,'wsh'=4] {'seq'}, use_global_device_ids=true, to_apply=%region_31.32 | all-reduce | flops 3672 | bytes 29376 | tf_op jit(solution)/shard_map/psum | solution.py:245
  1427.2 72.2 %all-reduce.27.cloned.1.call-done = (f32[256,4384]{0,1:T(8,128)}, f32[512,1024]{1,0:T(8,128)}) async-done(((f32[256,4384]{0,1:T(8,128)}, f32[512,1024]{1,0:T(8,128)}), (f32[256,4384]{0,1:T(8,128)}, f32[512,1024]{1,0:T(8,128)})) %all-reduce.27.cloned.1.call-update) | async-done | bytes 6586384 | tf_op jit(solution)/shard_map/psum | solution.py:245
  (934 shorter events, 595.2 us)
Async XLA Ops:
  7.2 164.1 %all-gather.7.cloned.1.call-start = ((), (), s32[]{:S(2)}) async-start(), calls=%async_computation.10 | async-start | bytes 11223040 | tf_op jit(solution)/shard_map/all_gather | solution.py:112
  7.9 250.6 %all-gather.9.cloned.1.call-start = ((), (), s32[]{:S(2)}) async-start(), calls=%async_computation.11 | async-start | bytes 2359296 | tf_op jit(solution)/shard_map/all_gather | solution.py:156
  21.3 159.3 %copy-start.47 = (f32[4,1,256]{2,1,0:T(1,128)}, f32[4,1,256]{2,1,0:T(1,128)S(1)}, u32[]{:S(2)}) copy-start(f32[4,1,256]{2,1,0:T(1,128)S(1)} %convert_element_type.247) | copy-start | bytes 12292
  64.4 116.2 %copy-start.51 = (f32[512]{0:T(512)}, f32[512]{0:T(512)S(1)}, u32[]{:S(2)}) copy-start(f32[512]{0:T(512)S(1)} %fusion.140) | copy-start | bytes 6148
  64.4 132.9 %copy-start.37 = (f32[512]{0:T(512)}, f32[512]{0:T(512)S(1)}, u32[]{:S(2)}) copy-start(f32[512]{0:T(512)S(1)} %get-tuple-element.800) | copy-start | bytes 6148
  64.4 132.9 %copy-start.39 = (f32[512]{0:T(512)}, f32[512]{0:T(512)S(1)}, u32[]{:S(2)}) copy-start(f32[512]{0:T(512)S(1)} %get-tuple-element.801) | copy-start | bytes 6148
  64.5 132.9 %copy-start.41 = (f32[512]{0:T(512)}, f32[512]{0:T(512)S(1)}, u32[]{:S(2)}) copy-start(f32[512]{0:T(512)S(1)} %get-tuple-element.802) | copy-start | bytes 6148
  182.8 14.0 collective-permute-start
  204.3 9.6 all-to-all-start
  213.9 39.5 %copy-start.19 = (bf16[512,8,4]{0,2,1:T(4,128)(2,1)}, bf16[512,8,4]{0,2,1:T(4,128)(2,1)S(1)}, u32[]{:S(2)}) copy-start(bf16[512,8,4]{0,2,1:T(4,128)(2,1)S(1)} %all-to-all-done) | copy-start | bytes 98308
  213.9 36.4 %all-to-all-start.1 = ((bf16[8,512,256]{2,1,0:T(8,128)(2,1)}), bf16[8,512,256]{2,1,0:T(8,128)(2,1)S(1)}, u32[]{:S(2)}, u32[]{:S(2)}) async-start(bf16[8,512,256]{2,1,0:T(8,128)(2,1)} %fusion.121), calls=%async_computation.1 | async-start | bytes 4194304 | tf_op jit(solution)/shard_map/all_to_all | solution.py:13
  218.1 251.5 %all-gather.11.cloned.1.call-start = ((), (), s32[]{:S(2)}) async-start(), calls=%async_computation.12 | async-start | bytes 5242880 | tf_op jit(solution)/shard_map/all_gather | solution.py:113
  220.4 208.1 %copy-start.49 = (f32[256]{0:T(256)}, f32[256]{0:T(256)S(1)}, u32[]{:S(2)}) copy-start(f32[256]{0:T(256)S(1)} %mul.797) | copy-start | bytes 3076
  220.5 38.0 %copy-start.56 = (f32[4]{0:T(128)}, f32[4]{0:T(128)S(1)}, u32[]{:S(2)}) copy-start(f32[4]{0:T(128)S(1)} %fusion.142) | copy-start | bytes 52
  220.5 37.9 %copy-start.54 = (f32[4]{0:T(128)}, f32[4]{0:T(128)S(1)}, u32[]{:S(2)}) copy-start(f32[4]{0:T(128)S(1)} %dynamic-slice_convert_fusion.1) | copy-start | bytes 52
  220.8 37.7 %copy-start.17 = (f32[8,512,4]{1,2,0:T(4,128)}, f32[8,512,4]{1,2,0:T(4,128)S(1)}, u32[]{:S(2)}) copy-start(f32[8,512,4]{1,2,0:T(4,128)S(1)} %get-tuple-element.766) | copy-start | bytes 196612
  250.3 178.2 %copy-start.4 = (bf16[8,512,256]{2,1,0:T(8,128)(2,1)}, bf16[8,512,256]{2,1,0:T(8,128)(2,1)S(1)}, u32[]{:S(2)}) copy-start(bf16[8,512,256]{2,1,0:T(8,128)(2,1)S(1)} %all-to-all-done.1) | copy-start | bytes 6291460
  432.5 30.3 %all-to-all-start.2 = ((bf16[8,512,256]{2,1,0:T(8,128)(2,1)}), bf16[8,512,256]{2,1,0:T(8,128)(2,1)S(1)}, u32[]{:S(2)}, u32[]{:S(2)}) async-start(bf16[8,512,256]{2,1,0:T(8,128)(2,1)} %add_convert_fusion.1), calls=%async_computation.2 | async-start | bytes 4194304 | tf_op jit(solution)/shard_map/all_to_all | solution.py:178
  448.4 28.3 %copy-start.25 = (f32[4,1,512]{2,1,0:T(1,128)}, f32[4,1,512]{2,1,0:T(1,128)S(1)}, u32[]{:S(2)}) copy-start(f32[4,1,512]{2,1,0:T(1,128)S(1)} %convert_element_type.249) | copy-start | bytes 24580
  483.7 30.2 %all-to-all-start.3 = ((bf16[512,8,256]{2,0,1:T(8,128)(2,1)}), bf16[512,8,256]{2,0,1:T(8,128)(2,1)S(1)}, u32[]{:S(2)}, u32[]{:S(2)}) async-start(bf16[512,8,256]{2,0,1:T(8,128)(2,1)} %bitcast.441), calls=%async_computation.3 | async-start | bytes 4194304 | tf_op jit(solution)/shard_map/all_to_all | solution.py:199
  487.3 455.5 %reduce-scatter.7.cloned.1.call-start = ((), (), s32[]{:S(2)}) async-start(), calls=%async_computation.13 | async-start | bytes 2359296 | tf_op jit(solution)/shard_map/reduce_scatter | solution.py:213
  868.5 185.7 %reduce-scatter.11.cloned.1.call-start = ((), (), s32[]{:S(2)}) async-start(), calls=%async_computation.15 | async-start | bytes 10485760 | tf_op jit(solution)/shard_map/reduce_scatter | solution.py:261
  895.0 15.5 %all-to-all-start.5 = ((bf16[8,512,4]{1,2,0:T(4,128)(2,1)}), bf16[8,512,4]{1,2,0:T(4,128)(2,1)S(1)}, u32[]{:S(2)}, u32[]{:S(2)}) async-start(bf16[8,512,4]{1,2,0:T(4,128)(2,1)} %get-tuple-element.759), calls=%async_computation.6 | async-start | bytes 65536 | tf_op jit(solution)/shard_map/all_to_all | solution.py:209
  910.5 32.3 %copy-start.38 = (f32[512]{0:T(512)S(1)}, f32[512]{0:T(512)}, u32[]{:S(2)}) copy-start(f32[512]{0:T(512)} %copy-done.37) | copy-start | bytes 6148
  910.5 32.3 %copy-start.40 = (f32[512]{0:T(512)S(1)}, f32[512]{0:T(512)}, u32[]{:S(2)}) copy-start(f32[512]{0:T(512)} %copy-done.39) | copy-start | bytes 6148
  910.5 32.3 %copy-start.42 = (f32[512]{0:T(512)S(1)}, f32[512]{0:T(512)}, u32[]{:S(2)}) copy-start(f32[512]{0:T(512)} %copy-done.41) | copy-start | bytes 6148
  910.5 30.7 %all-to-all-start.4 = ((bf16[8,512,256]{2,1,0:T(8,128)(2,1)}), bf16[8,512,256]{2,1,0:T(8,128)(2,1)S(1)}, u32[]{:S(2)}, u32[]{:S(2)}) async-start(bf16[8,512,256]{2,1,0:T(8,128)(2,1)} %get-tuple-element.796), calls=%async_computation.4 | async-start | bytes 4194304 | tf_op jit(solution)/shard_map/all_to_all | solution.py:206
  914.6 441.7 %reduce-scatter.9.cloned.1.call-start = ((), (), s32[]{:S(2)}) async-start(), calls=%async_computation.14 | async-start | bytes 22446080 | tf_op jit(solution)/shard_map/reduce_scatter | solution.py:260
  957.0 3.8 collective-permute-start.1
  973.8 427.7 %reduce-scatter.13.cloned.1.call-start = ((), (), s32[]{:S(2)}) async-start(), calls=%async_computation.16 | async-start | bytes 1474560
  975.4 524.1 %all-reduce.27.cloned.1.call-start = ((), (), s32[]{:S(2)}) async-start(), calls=%async_computation.17 | async-start | bytes 13172736 | tf_op jit(solution)/shard_map/psum | solution.py:245
  1366.6 31.4 %copy-start.46 = (f32[512]{0:T(512)S(1)}, f32[512]{0:T(512)}, u32[]{:S(2)}) copy-start(f32[512]{0:T(512)} %copy-done.45) | copy-start | bytes 6148
  (126 other events, 1047.2 us)
Sparse Core Ops, SparseCore 0:
  9.5 161.6 all-gather.6
  203.7 38.3 all-gather.8
  243.6 79.8 all-gather.10
  868.7 38.6 reduce-scatter.6
  909.5 144.6 reduce-scatter.10
  1056.4 299.8 reduce-scatter.8
  1358.6 30.4 reduce-scatter.12
  1392.6 106.8 all-reduce.26
